TPU v7x, 32 devices: a whole 2x2x4 slice. The times are simulated.
32 devices in a mesh: vocab: 8 (over y, x, core), blk: 4 (over z).
Axes of the slice: x: 2, y: 2, z: 4, core: 2. Of those that a mesh axis runs over, the one named last changes fastest.
Arguments:
- char_ids: int32 [16384, 50], P(('vocab', 'blk')), may hold values from 0 to 255, as said below
- char_table: bfloat16 [256, 16], replicated, may hold values from -5 to 5
- conv_weight: bfloat16 [112, 896], replicated, may hold values from -0.75 to 0.75
- proj_weight: bfloat16 [896, 1024], replicated, may hold values from -0.1875 to 0.1875
- gate_weight: bfloat16 [2, 1024, 1024], replicated, may hold values from -0.1875 to 0.1875
- trans_weight: bfloat16 [2, 1024, 1024], replicated, may hold values from -0.1875 to 0.1875
- gate_bias: float32 [2, 1024], replicated, may hold values from -4 to 4
- hidden: bfloat16 [2048, 1024], P(('vocab', 'blk')), may hold values from -48 to 48
- targets: int32 [2048], P(('vocab', 'blk')), may hold values from 0 to 16383
Outputs:
- row_loss: float32 [2048], P(('vocab', 'blk'))
- hidden_grad: bfloat16 [2048, 1024], P(('vocab', 'blk'))
Inputs may be any that keep to these rules, and one draw needn't show every extreme that they name: `char_ids`: each word has 2 to 50 characters with ids 1 and up, followed by the padding id 0.
All inputs are finite; a program needn't handle non-finite values.
Results may differ from a plain program's by a relative error of at most 0.014.
The roundings to bfloat16 on the way count: a program that leaves them out, or rounds other values in their place, can miss the bound.
Values may be sent and summed in bfloat16 or wider, within the bound.
No kernel may reach another device: no remote copies, remote signals or barrier semaphores. Data moves between devices by JAX's collectives and lax.ppermute only.
A program may use at most 128 MiB of HBM per device.

v0:
```python
import math
import jax
import jax.numpy as jnp
from jax import lax
from jax.sharding import PartitionSpec as P


def shifted(array, axis, by):
    count = lax.axis_size(axis)
    return lax.ppermute(array, axis, [(i, (i + by) % count) for i in range(count)])


def char_features(char_ids, char_table, conv_weight):
    num_words = char_ids.shape[0]
    length = char_ids.shape[1]
    symbols = char_table.shape[0]
    embed_dim = char_table.shape[1]
    widths = conv_weight.shape[0] // embed_dim
    filters = conv_weight.shape[1] // widths
    onehot = (char_ids[:, :, None] == jnp.arange(symbols, dtype=jnp.int32)[None, None, :]).astype(
        jnp.bfloat16
    )
    vectors = jnp.dot(
        onehot.reshape(num_words * length, symbols), char_table, preferred_element_type=jnp.float32
    )
    vectors = vectors.astype(jnp.bfloat16).reshape(num_words, length, embed_dim)
    padded = jnp.pad(vectors, ((0, 0), (0, widths - 1), (0, 0)))
    windows = jnp.concatenate(
        [padded[:, shift_at : shift_at + length, :] for shift_at in range(widths)], axis=2
    )
    offset = jnp.arange(widths * embed_dim) // embed_dim
    kernel = jnp.arange(widths * filters) // filters + 1
    masked = jnp.where(offset[:, None] < kernel[None, :], conv_weight, jnp.zeros_like(conv_weight))
    conv_out = jnp.dot(
        windows.reshape(num_words * length, widths * embed_dim),
        masked,
        preferred_element_type=jnp.float32,
    )
    conv_out = conv_out.reshape(num_words, length, widths * filters)
    position = jnp.arange(length)
    usable = position[:, None] <= length - kernel[None, :]
    pooled = jnp.max(jnp.where(usable[None, :, :], conv_out, -jnp.inf), axis=1)
    return jnp.tanh(pooled).astype(jnp.bfloat16)


def embed_words(
    char_ids, char_table, conv_weight, proj_weight, gate_weight, trans_weight, gate_bias
):
    features = char_features(char_ids, char_table, conv_weight)
    current = jnp.dot(features, proj_weight, preferred_element_type=jnp.float32).astype(
        jnp.bfloat16
    )
    for layer_idx in range(gate_weight.shape[0]):
        opened = jax.nn.sigmoid(
            jnp.dot(current, gate_weight[layer_idx], preferred_element_type=jnp.float32)
            + gate_bias[layer_idx]
        )
        carried = jax.nn.relu(
            jnp.dot(current, trans_weight[layer_idx], preferred_element_type=jnp.float32)
        )
        current = (opened * carried + (1.0 - opened) * current.astype(jnp.float32)).astype(
            jnp.bfloat16
        )
    return current


def embed_all(char_ids, char_table, conv_weight, proj_weight, gate_weight, trans_weight, gate_bias):
    num_total = char_ids.shape[0]
    block_size = math.gcd(num_total, 128)
    grouped = char_ids.reshape(num_total // block_size, block_size, char_ids.shape[1])

    def one_block(piece_ids):
        return embed_words(
            piece_ids, char_table, conv_weight, proj_weight, gate_weight, trans_weight, gate_bias
        )

    return lax.map(one_block, grouped).reshape(num_total, proj_weight.shape[1])


def pick_targets(word_panel, row_spot):
    count_words = word_panel.shape[0]
    inside = (row_spot >= 0) & (row_spot < count_words)
    picked = jnp.take(word_panel, jnp.clip(row_spot, 0, count_words - 1), axis=0).astype(
        jnp.float32
    )
    return jnp.where(inside[:, None], picked, jnp.zeros_like(picked))


def fold_panel(acc_state, row_block, row_spot, word_panel):
    run_max, run_total, weighted, target_vec = acc_state
    scores = lax.dot_general(
        row_block, word_panel, (((1,), (1,)), ((), ())), preferred_element_type=jnp.float32
    )
    new_max = jnp.maximum(run_max, jnp.max(scores, axis=1))
    rescale = jnp.exp(run_max - new_max)
    soft_weights = jnp.exp(scores - new_max[:, None]).astype(jnp.bfloat16)
    run_total = run_total * rescale + jnp.sum(soft_weights.astype(jnp.float32), axis=1)
    weighted = weighted * rescale[:, None] + jnp.dot(
        soft_weights, word_panel, preferred_element_type=jnp.float32
    )
    target_vec = target_vec + pick_targets(word_panel, row_spot)
    return (new_max, run_total, weighted, target_vec)


def finish_rows(hidden, run_max, run_total, weighted, target_vec):
    target_score = jnp.sum(hidden.astype(jnp.float32) * target_vec, axis=1)
    row_loss = run_max + jnp.log(run_total) - target_score
    hidden_grad = (weighted / run_total[:, None] - target_vec).astype(jnp.bfloat16)
    return (row_loss, hidden_grad)


def per_device(
    char_ids,
    char_table,
    conv_weight,
    proj_weight,
    gate_weight,
    trans_weight,
    gate_bias,
    hidden,
    targets,
):
    embeds = embed_all(
        char_ids, char_table, conv_weight, proj_weight, gate_weight, trans_weight, gate_bias
    )
    local_words = embeds.shape[0]
    my_rows = hidden.shape[0]
    model_dim = hidden.shape[1]
    blocks = lax.axis_size("blk")
    group_idx = lax.axis_index("blk")
    word_panel = lax.all_gather(embeds, "vocab", axis=0, tiled=True)
    group_hidden = lax.all_gather(hidden, "blk", axis=0, tiled=True)
    group_goal = lax.all_gather(targets, "blk", axis=0, tiled=True)
    owner_dev = group_goal // local_words
    in_group = owner_dev % blocks == group_idx
    spot_all = jnp.where(in_group, owner_dev // blocks * local_words + group_goal % local_words, -1)
    running = (
        jnp.full((my_rows,), -jnp.inf, jnp.float32),
        jnp.zeros((my_rows,), jnp.float32),
        jnp.zeros((my_rows, model_dim), jnp.float32),
        jnp.zeros((my_rows, model_dim), jnp.float32),
    )
    for step_idx in range(blocks):
        which_block = (group_idx - step_idx) % blocks
        row_block = lax.dynamic_slice_in_dim(group_hidden, which_block * my_rows, my_rows, 0)
        row_spot = lax.dynamic_slice_in_dim(spot_all, which_block * my_rows, my_rows, 0)
        running = fold_panel(running, row_block, row_spot, word_panel)
        running = shifted((running[0], running[1], running[2], running[3]), "blk", 1)
    run_max, run_total, weighted, target_vec = running
    return finish_rows(hidden, run_max, run_total, weighted, target_vec)


def solution(mesh):
    return jax.shard_map(
        per_device,
        mesh=mesh,
        in_specs=(
            P(("vocab", "blk"), None),
            P(),
            P(),
            P(),
            P(),
            P(),
            P(),
            P(("vocab", "blk"), None),
            P(("vocab", "blk")),
        ),
        out_specs=(P(("vocab", "blk")), P(("vocab", "blk"), None)),
        check_vma=False,
    )
```

profile of v0, /device:TPU:0, one launch (start us, length us, event | category | flops | bytes accessed | tf_op | source)
XLA Modules:
  0.0 273.5 jit_solution(3712595097836582395)
XLA Ops:
  8.3 100.8 %while.13 = (s32[]{:T(128)}, bf16[4,128,1024]{2,1,0:T(8,128)(2,1)}, s32[4,128,50]{2,1,0:T(8,128)S(1)}, bf16[256,16]{0,1:T(8,128)(2,1)}, bf16[112,896]{1,0:T(8,12...) while((s32[]{:T(128)}, bf16[4,128,1024]{2,1,0:T(8,128)(2,1)}, ...), condition=%wide.region_2.3_spmd, body=%wide.region_0.2_spmd.sunk | while | flops 2662044928 | bytes 67010176 | solution.py:77
  8.5 4.2 %convolution_convert_fusion.4 = bf16[6400,16]{0,1:T(8,128)(2,1)S(1)} fusion(bf16[256,16]{0,1:T(8,128)(2,1)} %get-tuple-element.308, s32[6400]{0:T(1024)S(1)} %eq.53), kind=kOutput, calls=%fused_computation.5.clone.1 | convolution fusion | flops 54169600 | bytes 238592 | tf_op jit(solution)/shard_map/while/body/eval_jaxpr/dot_general | solution.py:23
  12.7 1.5 concatenate.12
  15.2 1.7 pad_slice_fusion.7
  16.9 1.4 copy.29
  24.2 4.8 %select_reduce_fusion.2 = f32[128,896]{1,0:T(8,128)S(1)} fusion(pred[50,896]{1,0:T(8,128)(4,1)S(1)} %iota_compare_fusion.6, bf16[128,50,112]{0,2,1:T(8,128)(2,1)} %constant_dynamic-update-slice_fusion.20, bf16[112,896]{1,0:T(8,128)(2,1)S(1)} %copy-done.9, s32[896]{0:T(1024)S(1)} %fusion.150, s32[112]{0:T(128)S(1)} %and_select_fusion.6), kind=kOutput, calls=%fused_computation.4.clone.1 | convolution fusion | flops 1296060416 | bytes 2141888 | tf_op jit(solution)/shard_map/while/body/eval_jaxpr/dot_general | solution.py:34
  33.7 4.2 %convolution_convert_fusion.4 = bf16[6400,16]{0,1:T(8,128)(2,1)S(1)} fusion(bf16[256,16]{0,1:T(8,128)(2,1)} %get-tuple-element.308, s32[6400]{0:T(1024)S(1)} %eq.53), kind=kOutput, calls=%fused_computation.5.clone.1 | convolution fusion | flops 54169600 | bytes 238592 | tf_op jit(solution)/shard_map/while/body/eval_jaxpr/dot_general | solution.py:23
  37.9 1.5 concatenate.12
  40.4 1.7 pad_slice_fusion.7
  42.0 1.4 copy.29
  49.4 4.8 %select_reduce_fusion.2 = f32[128,896]{1,0:T(8,128)S(1)} fusion(pred[50,896]{1,0:T(8,128)(4,1)S(1)} %iota_compare_fusion.6, bf16[128,50,112]{0,2,1:T(8,128)(2,1)} %constant_dynamic-update-slice_fusion.20, bf16[112,896]{1,0:T(8,128)(2,1)S(1)} %copy-done.9, s32[896]{0:T(1024)S(1)} %fusion.150, s32[112]{0:T(128)S(1)} %and_select_fusion.6), kind=kOutput, calls=%fused_computation.4.clone.1 | convolution fusion | flops 1296060416 | bytes 2141888 | tf_op jit(solution)/shard_map/while/body/eval_jaxpr/dot_general | solution.py:34
  58.9 4.2 %convolution_convert_fusion.4 = bf16[6400,16]{0,1:T(8,128)(2,1)S(1)} fusion(bf16[256,16]{0,1:T(8,128)(2,1)} %get-tuple-element.308, s32[6400]{0:T(1024)S(1)} %eq.53), kind=kOutput, calls=%fused_computation.5.clone.1 | convolution fusion | flops 54169600 | bytes 238592 | tf_op jit(solution)/shard_map/while/body/eval_jaxpr/dot_general | solution.py:23
  63.1 1.5 concatenate.12
  65.6 1.7 pad_slice_fusion.7
  67.2 1.4 copy.29
  74.6 4.8 %select_reduce_fusion.2 = f32[128,896]{1,0:T(8,128)S(1)} fusion(pred[50,896]{1,0:T(8,128)(4,1)S(1)} %iota_compare_fusion.6, bf16[128,50,112]{0,2,1:T(8,128)(2,1)} %constant_dynamic-update-slice_fusion.20, bf16[112,896]{1,0:T(8,128)(2,1)S(1)} %copy-done.9, s32[896]{0:T(1024)S(1)} %fusion.150, s32[112]{0:T(128)S(1)} %and_select_fusion.6), kind=kOutput, calls=%fused_computation.4.clone.1 | convolution fusion | flops 1296060416 | bytes 2141888 | tf_op jit(solution)/shard_map/while/body/eval_jaxpr/dot_general | solution.py:34
  84.1 4.2 %convolution_convert_fusion.4 = bf16[6400,16]{0,1:T(8,128)(2,1)S(1)} fusion(bf16[256,16]{0,1:T(8,128)(2,1)} %get-tuple-element.308, s32[6400]{0:T(1024)S(1)} %eq.53), kind=kOutput, calls=%fused_computation.5.clone.1 | convolution fusion | flops 54169600 | bytes 238592 | tf_op jit(solution)/shard_map/while/body/eval_jaxpr/dot_general | solution.py:23
  88.3 1.5 concatenate.12
  90.8 1.7 pad_slice_fusion.7
  99.8 4.8 %select_reduce_fusion.2 = f32[128,896]{1,0:T(8,128)S(1)} fusion(pred[50,896]{1,0:T(8,128)(4,1)S(1)} %iota_compare_fusion.6, bf16[128,50,112]{0,2,1:T(8,128)(2,1)} %constant_dynamic-update-slice_fusion.20, bf16[112,896]{1,0:T(8,128)(2,1)S(1)} %copy-done.9, s32[896]{0:T(1024)S(1)} %fusion.150, s32[112]{0:T(128)S(1)} %and_select_fusion.6), kind=kOutput, calls=%fused_computation.4.clone.1 | convolution fusion | flops 1296060416 | bytes 2141888 | tf_op jit(solution)/shard_map/while/body/eval_jaxpr/dot_general | solution.py:34
  110.7 9.9 %all-reduce.1 = s32[256]{0:T(256)S(1)} all-reduce(s32[256]{0:T(256)S(1)} %dynamic-update-slice), channel_id=1, replica_groups=mesh['vocab'=8,'blk'=4] {'blk'}, use_global_device_ids=true, to_apply=%add.1 | all-reduce | flops 256 | bytes 2048
  121.3 15.9 %all_gather.9 = bf16[256,1024]{1,0:T(8,128)(2,1)S(1)} all-gather(bf16[64,1024]{1,0:T(8,128)(2,1)} %param.20), channel_id=1, replica_groups=mesh['vocab'=8,'blk'=4] {'blk'}, dimensions={0}, use_global_device_ids=true | all-gather | bytes 655360 | tf_op jit(solution)/shard_map/all_gather | solution.py:132
  137.3 29.1 %all-gather.2.cloned.1.call-done = bf16[4096,1024]{1,0:T(8,128)(2,1)} async-done(((bf16[512,1024]{1,0:T(8,128)(2,1)}), bf16[4096,1024]{1,0:T(8,128)(2,1)}) %all-gather.2.cloned.1.call-update) | async-done | bytes 8388624 | tf_op jit(solution)/shard_map/all_gather | solution.py:131
  166.3 5.3 %gather_fusion = bf16[64,1024]{1,0:T(8,128)(2,1)S(1)} fusion(bf16[4096,1024]{1,0:T(8,128)(2,1)} %all-gather.2.cloned.1.call-done, s32[1024]{0:T(1024)S(1)} %pad_clamp_fusion.3), kind=kCustom, calls=%fused_computation.clone | custom fusion | bytes 262400 | tf_op jit(solution)/shard_map/jit(_take)/gather | solution.py:83
  172.4 1.5 collective-permute-start.8
  173.9 6.7 %fusion.101 = (f32[64]{0:T(128)S(1)}, f32[64,4096]{1,0:T(8,128)S(1)}) fusion(bf16[4096,1024]{1,0:T(8,128)(2,1)} %all-gather.2.cloned.1.call-done, bf16[256,1024]{1,0:T(8,128)(2,1)S(1)} %all_gather.9, s32[]{:T(128)S(6)} %select_n.128), kind=kOutput, calls=%fused_computation.147 | convolution fusion | flops 537132992 | bytes 9568516 | tf_op jit(solution)/shard_map/dot_general | solution.py:91
  180.6 1.5 collective-permute-start
  183.1 2.4 convolution_add_fusion
  185.5 1.5 collective-permute-start.12
  187.1 3.3 %fusion.102 = (f32[64]{0:T(128)}, f32[64,4096]{1,0:T(8,128)S(1)}) fusion(bf16[4096,1024]{1,0:T(8,128)(2,1)S(1)} %copy-done, bf16[256,1024]{1,0:T(8,128)(2,1)S(1)} %all_gather.9, s32[]{:T(128)S(6)} %select_n.130), kind=kOutput, calls=%fused_computation.148 | convolution fusion | flops 537132992 | bytes 9568516 | tf_op jit(solution)/shard_map/dot_general | solution.py:91
  190.4 3.3 %fusion.103 = (f32[64]{0:T(128)}, f32[64,4096]{1,0:T(8,128)S(1)}) fusion(bf16[4096,1024]{1,0:T(8,128)(2,1)S(1)} %copy-done, bf16[256,1024]{1,0:T(8,128)(2,1)S(1)} %all_gather.9, s32[]{:T(128)S(6)} %select_n.132), kind=kOutput, calls=%fused_computation.149 | convolution fusion | flops 537132992 | bytes 9568516 | tf_op jit(solution)/shard_map/dot_general | solution.py:91
  193.6 4.2 %fusion.104 = (f32[64]{0:T(128)}, f32[64,4096]{1,0:T(8,128)S(1)}) fusion(bf16[4096,1024]{1,0:T(8,128)(2,1)S(1)} %copy-done, bf16[256,1024]{1,0:T(8,128)(2,1)} %copy-done.2, s32[]{:T(128)S(6)} %select_n.134), kind=kOutput, calls=%fused_computation.150 | convolution fusion | flops 537132992 | bytes 9568516 | tf_op jit(solution)/shard_map/dot_general | solution.py:91
  197.8 5.3 %gather_fusion.1 = bf16[64,1024]{1,0:T(8,128)(2,1)S(1)} fusion(bf16[4096,1024]{1,0:T(8,128)(2,1)} %all-gather.2.cloned.1.call-done, s32[1024]{0:T(1024)S(1)} %pad_clamp_fusion.2), kind=kCustom, calls=%fused_computation.1.clone | custom fusion | bytes 262400 | tf_op jit(solution)/shard_map/jit(_take)/gather | solution.py:83
  203.0 5.3 %gather_fusion.2 = bf16[64,1024]{1,0:T(8,128)(2,1)S(1)} fusion(bf16[4096,1024]{1,0:T(8,128)(2,1)} %all-gather.2.cloned.1.call-done, s32[1024]{0:T(1024)S(1)} %pad_clamp_fusion.1), kind=kCustom, calls=%fused_computation.2.clone | custom fusion | bytes 262400 | tf_op jit(solution)/shard_map/jit(_take)/gather | solution.py:83
  208.3 5.3 %gather_fusion.3 = bf16[64,1024]{1,0:T(8,128)(2,1)S(1)} fusion(bf16[4096,1024]{1,0:T(8,128)(2,1)} %all-gather.2.cloned.1.call-done, s32[1024]{0:T(1024)S(1)} %pad_clamp_fusion), kind=kCustom, calls=%fused_computation.3.clone | custom fusion | bytes 262400 | tf_op jit(solution)/shard_map/jit(_take)/gather | solution.py:83
  214.2 1.9 collective-permute-start.1
  217.0 1.5 collective-permute-start.5
  221.0 1.4 collective-permute-done.5
  222.4 3.1 %collective-permute-done.2 = f32[64]{0:T(128)S(1)} collective-permute-done((f32[64]{0:T(128)S(1)}, f32[64]{0:T(128)S(1)}, u32[]{:S(2)}, u32[]{:S(2)}) %collective-permute-start.2) | collective-permute-done | bytes 288 | tf_op jit(solution)/shard_map/ppermute | solution.py:10
  227.5 5.2 %multiply_add_fusion.2 = f32[64,1024]{1,0:T(8,128)S(1)} fusion(f32[64,1024]{1,0:T(8,128)} %collective-permute-done.12, f32[64]{0:T(128)S(1)} %get-tuple-element.173, bf16[4096,1024]{1,0:T(8,128)(2,1)} %all-gather.2.cloned.1.call-done, f32[64,4096]{1,0:T(8,128)S(1)} %get-tuple-element.209, f32[64]{0:T(128)S(1)} %max.43), kind=kOutput, calls=%fused_computation.88 | convolution fusion | flops 537526272 | bytes 9961984 | tf_op jit(solution)/shard_map/dot_general | solution.py:98
  233.0 4.1 %collective-permute-done.9 = f32[64,1024]{1,0:T(8,128)S(1)} collective-permute-done((f32[64,1024]{1,0:T(8,128)S(1)}, f32[64,1024]{1,0:T(8,128)S(1)}, u32[]{:S(2)}, u32[]{:S(2)}) %collective-permute-start.9) | collective-permute-done | bytes 262176 | tf_op jit(solution)/shard_map/ppermute | solution.py:10
  237.3 6.5 %collective-permute-done.13 = f32[64,1024]{1,0:T(8,128)S(1)} collective-permute-done((f32[64,1024]{1,0:T(8,128)S(1)}, f32[64,1024]{1,0:T(8,128)S(1)}, u32[]{:S(2)}, u32[]{:S(2)}) %collective-permute-start.13) | collective-permute-done | bytes 262176 | tf_op jit(solution)/shard_map/ppermute | solution.py:10
  243.7 1.7 multiply_add_fusion.1
  245.5 3.1 %collective-permute-done.10 = f32[64,1024]{1,0:T(8,128)S(1)} collective-permute-done((f32[64,1024]{1,0:T(8,128)S(1)}, f32[64,1024]{1,0:T(8,128)S(1)}, u32[]{:S(2)}, u32[]{:S(2)}) %collective-permute-start.10) | collective-permute-done | bytes 262176 | tf_op jit(solution)/shard_map/ppermute | solution.py:10
  248.8 6.4 %collective-permute-done.14 = f32[64,1024]{1,0:T(8,128)S(1)} collective-permute-done((f32[64,1024]{1,0:T(8,128)S(1)}, f32[64,1024]{1,0:T(8,128)S(1)}, u32[]{:S(2)}, u32[]{:S(2)}) %collective-permute-start.14) | collective-permute-done | bytes 262176 | tf_op jit(solution)/shard_map/ppermute | solution.py:10
  255.2 1.7 multiply_add_fusion
  257.2 2.5 collective-permute-start.3
  259.7 5.6 %collective-permute-done.7 = f32[64]{0:T(128)S(1)} collective-permute-done((f32[64]{0:T(128)S(1)}, f32[64]{0:T(128)S(1)}, u32[]{:S(2)}, u32[]{:S(2)}) %collective-permute-start.7) | collective-permute-done | bytes 288 | tf_op jit(solution)/shard_map/ppermute | solution.py:10
  (209 shorter events, 60.4 us)
Async XLA Ops:
  7.2 159.2 %all-gather.2.cloned.1.call-start = ((), (), s32[]{:S(2)}) async-start(), calls=%async_computation | async-start | bytes 9437184 | tf_op jit(solution)/shard_map/all_gather | solution.py:131
  8.2 100.9 %copy-start.11 = (u32[32]{0:T(128)S(1)}, u32[32]{0:T(128)}, u32[]{:S(2)}) copy-start(u32[32]{0:T(128)} %constant.224) | copy-start | bytes 388
  8.3 102.2 %copy-start.10 = (s32[64]{0:T(128)S(1)}, s32[64]{0:T(128)}, u32[]{:S(2)}) copy-start(s32[64]{0:T(128)} %param.21) | copy-start | bytes 772
  16.9 7.3 %copy-start.9 = (bf16[112,896]{1,0:T(8,128)(2,1)S(1)}, bf16[112,896]{1,0:T(8,128)(2,1)}, u32[]{:S(2)}) copy-start(bf16[112,896]{1,0:T(8,128)(2,1)} %get-tuple-element.309) | copy-start | bytes 602116 | tf_op jit(solution)/shard_map/while
  24.1 4.9 %copy-start.1 = (bf16[896,1024]{1,0:T(8,128)(2,1)S(1)}, bf16[896,1024]{1,0:T(8,128)(2,1)}, u32[]{:S(2)}) copy-start(bf16[896,1024]{1,0:T(8,128)(2,1)} %get-tuple-element.310) | copy-start | bytes 5505028 | tf_op jit(solution)/shard_map/while
  24.2 5.3 %copy-start.4 = (f32[2,1024]{1,0:T(2,128)S(1)}, f32[2,1024]{1,0:T(2,128)}, u32[]{:S(2)}) copy-start(f32[2,1024]{1,0:T(2,128)} %get-tuple-element.312) | copy-start | bytes 24580 | tf_op jit(solution)/shard_map/while
  24.2 5.3 %copy-start.7 = (bf16[2,1024,1024]{2,1,0:T(8,128)(2,1)S(1)}, bf16[2,1024,1024]{2,1,0:T(8,128)(2,1)}, u32[]{:S(2)}) copy-start(bf16[2,1024,1024]{2,1,0:T(8,128)(2,1)} %get-tuple-element.311) | copy-start | bytes 12582916 | tf_op jit(solution)/shard_map/while
  29.0 2.2 copy-start.8
  42.0 7.3 %copy-start.9 = (bf16[112,896]{1,0:T(8,128)(2,1)S(1)}, bf16[112,896]{1,0:T(8,128)(2,1)}, u32[]{:S(2)}) copy-start(bf16[112,896]{1,0:T(8,128)(2,1)} %get-tuple-element.309) | copy-start | bytes 602116 | tf_op jit(solution)/shard_map/while
  49.3 4.9 %copy-start.1 = (bf16[896,1024]{1,0:T(8,128)(2,1)S(1)}, bf16[896,1024]{1,0:T(8,128)(2,1)}, u32[]{:S(2)}) copy-start(bf16[896,1024]{1,0:T(8,128)(2,1)} %get-tuple-element.310) | copy-start | bytes 5505028 | tf_op jit(solution)/shard_map/while
  49.3 5.3 %copy-start.4 = (f32[2,1024]{1,0:T(2,128)S(1)}, f32[2,1024]{1,0:T(2,128)}, u32[]{:S(2)}) copy-start(f32[2,1024]{1,0:T(2,128)} %get-tuple-element.312) | copy-start | bytes 24580 | tf_op jit(solution)/shard_map/while
  49.3 5.3 %copy-start.7 = (bf16[2,1024,1024]{2,1,0:T(8,128)(2,1)S(1)}, bf16[2,1024,1024]{2,1,0:T(8,128)(2,1)}, u32[]{:S(2)}) copy-start(bf16[2,1024,1024]{2,1,0:T(8,128)(2,1)} %get-tuple-element.311) | copy-start | bytes 12582916 | tf_op jit(solution)/shard_map/while
  54.2 2.2 copy-start.8
  67.2 7.3 %copy-start.9 = (bf16[112,896]{1,0:T(8,128)(2,1)S(1)}, bf16[112,896]{1,0:T(8,128)(2,1)}, u32[]{:S(2)}) copy-start(bf16[112,896]{1,0:T(8,128)(2,1)} %get-tuple-element.309) | copy-start | bytes 602116 | tf_op jit(solution)/shard_map/while
  74.5 4.9 %copy-start.1 = (bf16[896,1024]{1,0:T(8,128)(2,1)S(1)}, bf16[896,1024]{1,0:T(8,128)(2,1)}, u32[]{:S(2)}) copy-start(bf16[896,1024]{1,0:T(8,128)(2,1)} %get-tuple-element.310) | copy-start | bytes 5505028 | tf_op jit(solution)/shard_map/while
  74.5 5.3 %copy-start.4 = (f32[2,1024]{1,0:T(2,128)S(1)}, f32[2,1024]{1,0:T(2,128)}, u32[]{:S(2)}) copy-start(f32[2,1024]{1,0:T(2,128)} %get-tuple-element.312) | copy-start | bytes 24580 | tf_op jit(solution)/shard_map/while
  74.5 5.3 %copy-start.7 = (bf16[2,1024,1024]{2,1,0:T(8,128)(2,1)S(1)}, bf16[2,1024,1024]{2,1,0:T(8,128)(2,1)}, u32[]{:S(2)}) copy-start(bf16[2,1024,1024]{2,1,0:T(8,128)(2,1)} %get-tuple-element.311) | copy-start | bytes 12582916 | tf_op jit(solution)/shard_map/while
  79.4 2.2 copy-start.8
  92.4 7.3 %copy-start.9 = (bf16[112,896]{1,0:T(8,128)(2,1)S(1)}, bf16[112,896]{1,0:T(8,128)(2,1)}, u32[]{:S(2)}) copy-start(bf16[112,896]{1,0:T(8,128)(2,1)} %get-tuple-element.309) | copy-start | bytes 602116 | tf_op jit(solution)/shard_map/while
  99.7 4.9 %copy-start.1 = (bf16[896,1024]{1,0:T(8,128)(2,1)S(1)}, bf16[896,1024]{1,0:T(8,128)(2,1)}, u32[]{:S(2)}) copy-start(bf16[896,1024]{1,0:T(8,128)(2,1)} %get-tuple-element.310) | copy-start | bytes 5505028 | tf_op jit(solution)/shard_map/while
  99.7 5.3 %copy-start.4 = (f32[2,1024]{1,0:T(2,128)S(1)}, f32[2,1024]{1,0:T(2,128)}, u32[]{:S(2)}) copy-start(f32[2,1024]{1,0:T(2,128)} %get-tuple-element.312) | copy-start | bytes 24580 | tf_op jit(solution)/shard_map/while
  99.8 5.3 %copy-start.7 = (bf16[2,1024,1024]{2,1,0:T(8,128)(2,1)S(1)}, bf16[2,1024,1024]{2,1,0:T(8,128)(2,1)}, u32[]{:S(2)}) copy-start(bf16[2,1024,1024]{2,1,0:T(8,128)(2,1)} %get-tuple-element.311) | copy-start | bytes 12582916 | tf_op jit(solution)/shard_map/while
  104.6 2.2 copy-start.8
  137.3 53.1 %copy-start.2 = (bf16[256,1024]{1,0:T(8,128)(2,1)}, bf16[256,1024]{1,0:T(8,128)(2,1)S(1)}, u32[]{:S(2)}) copy-start(bf16[256,1024]{1,0:T(8,128)(2,1)S(1)} %all_gather.9) | copy-start | bytes 1572868
  172.4 10.7 %copy-start = (bf16[4096,1024]{1,0:T(8,128)(2,1)S(1)}, bf16[4096,1024]{1,0:T(8,128)(2,1)}, u32[]{:S(2)}) copy-start(bf16[4096,1024]{1,0:T(8,128)(2,1)} %all-gather.2.cloned.1.call-done) | copy-start | bytes 25165828
  172.4 53.7 %collective-permute-start.8 = (f32[64,1024]{1,0:T(8,128)}, f32[64,1024]{1,0:T(8,128)}, u32[]{:S(2)}, u32[]{:S(2)}) collective-permute-start(f32[64,1024]{1,0:T(8,128)} %convert_select_fusion), channel_id=1, source_target_pairs={{0,1},{1,2},{2,3},{3,0},{4,5},{5,6},{6,7},{7,4},{8,9},{9,10},{10,1... | collective-permute-start | bytes 786440 | tf_op jit(solution)/shard_map/ppermute | solution.py:10
  180.6 32.9 %collective-permute-start = (f32[64]{0:T(128)S(1)}, f32[64]{0:T(128)}, u32[]{:S(2)}, u32[]{:S(2)}) collective-permute-start(f32[64]{0:T(128)S(1)} %get-tuple-element.206), channel_id=1, source_target_pairs={{0,1},{1,2},{2,3},{3,0},{4,5},{5,6},{6,7},{7,4},{8,9},{9,10},{10,1... | collective-permute-start | bytes 776 | tf_op jit(solution)/shard_map/ppermute | solution.py:10
  185.5 41.9 %collective-permute-start.12 = (f32[64,1024]{1,0:T(8,128)}, f32[64,1024]{1,0:T(8,128)}, u32[]{:S(2)}, u32[]{:S(2)}) collective-permute-start(f32[64,1024]{1,0:T(8,128)} %convolution_add_fusion), channel_id=1, source_target_pairs={{0,1},{1,2},{2,3},{3,0},{4,5},{5,6},{6,7},{7,4},{8,9},{9,10},{10,1... | collective-permute-start | bytes 786440 | tf_op jit(solution)/shard_map/ppermute | solution.py:10
  187.0 29.4 %collective-permute-start.4 = (f32[64]{0:T(128)}, f32[64]{0:T(128)}, u32[]{:S(2)}, u32[]{:S(2)}) collective-permute-start(f32[64]{0:T(128)} %get-tuple-element.205), channel_id=1, source_target_pairs={{0,1},{1,2},{2,3},{3,0},{4,5},{5,6},{6,7},{7,4},{8,9},{9,10},{10,1... | collective-permute-start | bytes 776 | tf_op jit(solution)/shard_map/ppermute | solution.py:10
  214.2 5.3 %collective-permute-start.1 = (f32[64]{0:T(128)S(1)}, f32[64]{0:T(128)S(1)}, u32[]{:S(2)}, u32[]{:S(2)}) collective-permute-start(f32[64]{0:T(128)S(1)} %max.43), channel_id=1, source_target_pairs={{0,1},{1,2},{2,3},{3,0},{4,5},{5,6},{6,7},{7,4},{8,9},{9,10},{10,1... | collective-permute-start | bytes 776 | tf_op jit(solution)/shard_map/ppermute | solution.py:10
  217.0 5.3 %collective-permute-start.5 = (f32[64]{0:T(128)S(1)}, f32[64]{0:T(128)S(1)}, u32[]{:S(2)}, u32[]{:S(2)}) collective-permute-start(f32[64]{0:T(128)S(1)} %get-tuple-element.172), channel_id=1, source_target_pairs={{0,1},{1,2},{2,3},{3,0},{4,5},{5,6},{6,7},{7,4},{8,9},{9,10},{10,1... | collective-permute-start | bytes 776 | tf_op jit(solution)/shard_map/ppermute | solution.py:10
  220.2 5.3 %collective-permute-start.2 = (f32[64]{0:T(128)S(1)}, f32[64]{0:T(128)S(1)}, u32[]{:S(2)}, u32[]{:S(2)}) collective-permute-start(f32[64]{0:T(128)S(1)} %max.44), channel_id=1, source_target_pairs={{0,1},{1,2},{2,3},{3,0},{4,5},{5,6},{6,7},{7,4},{8,9},{9,10},{10,1... | collective-permute-start | bytes 776 | tf_op jit(solution)/shard_map/ppermute | solution.py:10
  220.6 23.1 %slice-start = ((s8[8388608]{0:T(1024)(128)(4,1)}), s8[4194304]{0:T(1024)(128)(4,1)S(1)}, s32[]{:S(2)}) async-start(s8[8388608]{0:T(1024)(128)(4,1)} %bitcast.111), calls=%async_computation.1 | async-start | bytes 8388608
  222.4 23.1 %collective-permute-start.6 = (f32[64]{0:T(128)S(1)}, f32[64]{0:T(128)S(1)}, u32[]{:S(2)}, u32[]{:S(2)}) collective-permute-start(f32[64]{0:T(128)S(1)} %get-tuple-element.170), channel_id=1, source_target_pairs={{0,1},{1,2},{2,3},{3,0},{4,5},{5,6},{6,7},{7,4},{8,9},{9,10},{10,1... | collective-permute-start | bytes 776 | tf_op jit(solution)/shard_map/ppermute | solution.py:10
  227.1 10.0 %collective-permute-start.9 = (f32[64,1024]{1,0:T(8,128)S(1)}, f32[64,1024]{1,0:T(8,128)S(1)}, u32[]{:S(2)}, u32[]{:S(2)}) collective-permute-start(f32[64,1024]{1,0:T(8,128)S(1)} %select_add_fusion.2), channel_id=1, source_target_pairs={{0,1},{1,2},{2,3},{3,0},{4,5},{5,6},{6,7},{7,4},{8,9},{9,10},{10,1... | collective-permute-start | bytes 786440 | tf_op jit(solution)/shard_map/ppermute | solution.py:10
  227.4 9.7 %copy-start.5 = (pred[64]{0:T(512)(128)(4,1)S(1)}, pred[64]{0:T(512)(128)(4,1)}, u32[]{:S(2)}) copy-start(pred[64]{0:T(512)(128)(4,1)} %get-tuple-element.195) | copy-start | bytes 196
  227.4 9.6 %copy-start.6 = (pred[64]{0:T(512)(128)(4,1)S(1)}, pred[64]{0:T(512)(128)(4,1)}, u32[]{:S(2)}) copy-start(pred[64]{0:T(512)(128)(4,1)} %get-tuple-element.198) | copy-start | bytes 196
  227.5 16.3 %slice-start.1 = ((s8[8388608]{0:T(1024)(128)(4,1)}), s8[4194304]{0:T(1024)(128)(4,1)S(1)}, s32[]{:S(2)}) async-start(s8[8388608]{0:T(1024)(128)(4,1)} %bitcast.111), calls=%async_computation.2 | async-start | bytes 8388608
  232.6 11.1 %collective-permute-start.13 = (f32[64,1024]{1,0:T(8,128)S(1)}, f32[64,1024]{1,0:T(8,128)S(1)}, u32[]{:S(2)}, u32[]{:S(2)}) collective-permute-start(f32[64,1024]{1,0:T(8,128)S(1)} %multiply_add_fusion.2), channel_id=1, source_target_pairs={{0,1},{1,2},{2,3},{3,0},{4,5},{5,6},{6,7},{7,4},{8,9},{9,10},{10,1... | collective-permute-start | bytes 786440 | tf_op jit(solution)/shard_map/ppermute | solution.py:10
  237.2 11.4 %collective-permute-start.10 = (f32[64,1024]{1,0:T(8,128)S(1)}, f32[64,1024]{1,0:T(8,128)S(1)}, u32[]{:S(2)}, u32[]{:S(2)}) collective-permute-start(f32[64,1024]{1,0:T(8,128)S(1)} %select_add_fusion.1), channel_id=1, source_target_pairs={{0,1},{1,2},{2,3},{3,0},{4,5},{5,6},{6,7},{7,4},{8,9},{9,10},{10,1... | collective-permute-start | bytes 786440 | tf_op jit(solution)/shard_map/ppermute | solution.py:10
  245.4 9.8 %collective-permute-start.14 = (f32[64,1024]{1,0:T(8,128)S(1)}, f32[64,1024]{1,0:T(8,128)S(1)}, u32[]{:S(2)}, u32[]{:S(2)}) collective-permute-start(f32[64,1024]{1,0:T(8,128)S(1)} %multiply_add_fusion.1), channel_id=1, source_target_pairs={{0,1},{1,2},{2,3},{3,0},{4,5},{5,6},{6,7},{7,4},{8,9},{9,10},{10,1... | collective-permute-start | bytes 786440 | tf_op jit(solution)/shard_map/ppermute | solution.py:10
  248.7 16.5 %collective-permute-start.11 = (f32[64,1024]{1,0:T(8,128)S(1)}, f32[64,1024]{1,0:T(8,128)S(1)}, u32[]{:S(2)}, u32[]{:S(2)}) collective-permute-start(f32[64,1024]{1,0:T(8,128)S(1)} %select_add_fusion), channel_id=1, source_target_pairs={{0,1},{1,2},{2,3},{3,0},{4,5},{5,6},{6,7},{7,4},{8,9},{9,10},{10,1... | collective-permute-start | bytes 786440 | tf_op jit(solution)/shard_map/ppermute | solution.py:10
  255.2 10.0 %copy-start.3 = (bf16[64,1024]{1,0:T(8,128)(2,1)S(1)}, bf16[64,1024]{1,0:T(8,128)(2,1)}, u32[]{:S(2)}) copy-start(bf16[64,1024]{1,0:T(8,128)(2,1)} %param.20) | copy-start | bytes 393220
  256.9 8.3 %collective-permute-start.15 = (f32[64,1024]{1,0:T(8,128)S(1)}, f32[64,1024]{1,0:T(8,128)S(1)}, u32[]{:S(2)}, u32[]{:S(2)}) collective-permute-start(f32[64,1024]{1,0:T(8,128)S(1)} %multiply_add_fusion), channel_id=1, source_target_pairs={{0,1},{1,2},{2,3},{3,0},{4,5},{5,6},{6,7},{7,4},{8,9},{9,10},{10,1... | collective-permute-start | bytes 786440 | tf_op jit(solution)/shard_map/ppermute | solution.py:10
  257.0 8.2 %collective-permute-start.7 = (f32[64]{0:T(128)S(1)}, f32[64]{0:T(128)S(1)}, u32[]{:S(2)}, u32[]{:S(2)}) collective-permute-start(f32[64]{0:T(128)S(1)} %get-tuple-element.168), channel_id=1, source_target_pairs={{0,1},{1,2},{2,3},{3,0},{4,5},{5,6},{6,7},{7,4},{8,9},{9,10},{10,1... | collective-permute-start | bytes 776 | tf_op jit(solution)/shard_map/ppermute | solution.py:10
  257.2 8.9 %collective-permute-start.3 = (f32[64]{0:T(128)S(1)}, f32[64]{0:T(128)S(1)}, u32[]{:S(2)}, u32[]{:S(2)}) collective-permute-start(f32[64]{0:T(128)S(1)} %max.45), channel_id=1, source_target_pairs={{0,1},{1,2},{2,3},{3,0},{4,5},{5,6},{6,7},{7,4},{8,9},{9,10},{10,1... | collective-permute-start | bytes 776 | tf_op jit(solution)/shard_map/ppermute | solution.py:10
Sparse Core Ops, SparseCore 0:
  109.2 57.0 all-gather.1
where the time goes:
time: 274 us; the launch traced here: 273 us
  matrix products  77.2 us (28%)
  local copies, waits for them, and re-layouts  74.1 us (27%)
  waiting for transfers between devices  60.3 us (22%)
  blocking collectives  25.8 us (9%)
  between operations  15.1 us (6%)
  starting transfers between devices  11.7 us (4%)
  other arithmetic  8.73 us (3%)
    ppermute x16, waiting for transfers between devices, shifted(): lax.ppermute(array, axis, [(i, (i + by) % count) for i in range(count)])  31.2 us
    all_gather x1, waiting for transfers between devices, per_device(): word_panel = lax.all_gather(embeds, 'vocab', axis=0, tiled=True)  29.1 us
    while x64, local copies, waits for them, and re-layouts  22.6 us
    gather x4, local copies, waits for them, and re-layouts, pick_targets(): jnp.take(word_panel, jnp.clip(row_spot, 0, count_words - 1), axis=0)  21 us
    dot_general x4, matrix products, char_features(): jnp.dot(windows.reshape(num_words * length, widths * embed_dim), masked,...  19.3 us
    slice x28, local copies, waits for them, and re-layouts, char_features(): padded[:, shift_at:shift_at + length, :]  17.8 us
    dot_general x4, matrix products, fold_panel(): lax.dot_general(row_block, word_panel, (((1,), (1,)), ((), ())), preferre...  17.4 us
    dot_general x4, matrix products, char_features(): jnp.dot(onehot.reshape(num_words * length, symbols), char_table, preferre...  16.7 us
  transfers between devices with their start and end apart: 17, of which 9 were waited for; matrix products, arithmetic and copies ran while one was open for 19% of the time, Pallas kernels for 0%

commit v1 on v0

--- a/solution.py
+++ b/solution.py
@@ -128,7 +128,15 @@
     model_dim = hidden.shape[1]
     blocks = lax.axis_size("blk")
     group_idx = lax.axis_index("blk")
-    word_panel = lax.all_gather(embeds, "vocab", axis=0, tiled=True)
+    count_2 = lax.axis_size("vocab")
+    current_2, shards = (embeds, [embeds])
+    for _ in range(count_2 - 1):
+        current_2 = lax.ppermute(
+            current_2, "vocab", [(i_2, (i_2 + 1) % count_2) for i_2 in range(count_2)]
+        )
+        shards.insert(0, current_2)
+    line = jnp.concatenate(shards, axis=0)
+    word_panel = jnp.roll(line, (lax.axis_index("vocab") + 1) * embeds.shape[0], axis=0)
     group_hidden = lax.all_gather(hidden, "blk", axis=0, tiled=True)
     group_goal = lax.all_gather(targets, "blk", axis=0, tiled=True)
     owner_dev = group_goal // local_words

time: 274 us -> 373 us (1.36)
  waiting for transfers between devices: 60.3 us -> 124 us
  local copies, waits for them, and re-layouts: 74.1 us -> 119 us
  between operations: 15.1 us -> 1.62 us
  matrix products: 77.2 us -> 82 us
    ppermute x0 -> x7, waiting for transfers between devices: none -> 91.3 us  [per_device(): lax.ppermute(current_2, 'vocab', [(i_2, (i_2 + 1) % count_2) for i_2 in r...]
    all_gather x1 -> x0, waiting for transfers between devices: 29.1 us -> none  [per_device(): word_panel = lax.all_gather(embeds, 'vocab', axis=0, tiled=True)]
    unnamed x22 -> x47, local copies, waits for them, and re-layouts: 1.9 us -> 27.5 us
    dynamic_slice x0 -> x1, local copies, waits for them, and re-layouts: none -> 7.62 us  [per_device(): jnp.roll(line, (lax.axis_index('vocab') + 1) * embeds.shape[0], axis=0)]
    while x64 -> x72, local copies, waits for them, and re-layouts: 22.6 us -> 28.6 us
    slice x28, local copies, waits for them, and re-layouts: 17.8 us -> 23.2 us  [char_features(): padded[:, shift_at:shift_at + length, :]]
  transfers between devices with their start and end apart: 17 -> 23, of which waited for: 9 -> 15; matrix products, arithmetic and copies ran while one was open for 19% -> 11% of each run, Pallas kernels for 0% -> 0%
where the time goes in v1:
time: 373 us; the launch traced here: 372 us
  waiting for transfers between devices  124 us (33%)
  local copies, waits for them, and re-layouts  119 us (32%)
  matrix products  82 us (22%)
  blocking collectives  25 us (7%)
  other arithmetic  10 us (3%)
  starting transfers between devices  9.09 us (2%)
    ppermute x7, waiting for transfers between devices, per_device(): lax.ppermute(current_2, 'vocab', [(i_2, (i_2 + 1) % count_2) for i_2 in r...  91.3 us
    ppermute x16, waiting for transfers between devices, shifted(): lax.ppermute(array, axis, [(i, (i + by) % count) for i in range(count)])  32.9 us
    while x72, local copies, waits for them, and re-layouts  28.6 us
    unnamed x47, local copies, waits for them, and re-layouts  27.5 us
    slice x28, local copies, waits for them, and re-layouts, char_features(): padded[:, shift_at:shift_at + length, :]  23.2 us
    gather x4, local copies, waits for them, and re-layouts, pick_targets(): jnp.take(word_panel, jnp.clip(row_spot, 0, count_words - 1), axis=0)  21 us
    dot_general x4, matrix products, char_features(): jnp.dot(windows.reshape(num_words * length, widths * embed_dim), masked,...  20.5 us
    dot_general x4, matrix products, fold_panel(): lax.dot_general(row_block, word_panel, (((1,), (1,)), ((), ())), preferre...  17.3 us
  transfers between devices with their start and end apart: 23, of which 15 were waited for; matrix products, arithmetic and copies ran while one was open for 11% of the time, Pallas kernels for 0%

profile of v1, /device:TPU:0, one launch (start us, length us, event | category | flops | bytes accessed | tf_op | source)
XLA Modules:
  0.0 371.9 jit_solution(16271750154902497822)
XLA Ops:
  1.7 113.2 %while.13 = (s32[]{:T(128)}, bf16[4,128,1024]{2,1,0:T(8,128)(2,1)}, s32[4,128,50]{2,1,0:T(8,128)S(1)}, bf16[256,16]{0,1:T(8,128)(2,1)}, bf16[112,896]{1,0:T(8,12...) while((s32[]{:T(128)}, bf16[4,128,1024]{2,1,0:T(8,128)(2,1)}, ...), condition=%wide.region_2.3_spmd, body=%wide.region_0.2_spmd.sunk | while | flops 2662044928 | bytes 67026588 | solution.py:77
  2.6 4.2 %convolution_convert_fusion.4 = bf16[6400,16]{0,1:T(8,128)(2,1)S(1)} fusion(bf16[256,16]{0,1:T(8,128)(2,1)} %get-tuple-element.308, s32[6400]{0:T(1024)S(1)} %eq.56), kind=kOutput, calls=%fused_computation.5.clone.1 | convolution fusion | flops 54169600 | bytes 238592 | tf_op jit(solution)/shard_map/while/body/eval_jaxpr/dot_general | solution.py:23
  15.0 1.8 constant_dynamic-update-slice_fusion.33
  21.5 5.1 %select_reduce_fusion.2 = f32[128,896]{1,0:T(8,128)S(1)} fusion(pred[50,896]{1,0:T(8,128)(4,1)S(1)} %iota_compare_fusion.6, bf16[128,50,112]{0,2,1:T(8,128)(2,1)} %constant_dynamic-update-slice_fusion.36, bf16[112,896]{1,0:T(8,128)(2,1)} %get-tuple-element.309, s32[896]{0:T(1024)S(1)} %fusion.150, s32[112]{0:T(128)S(1)} %and_select_fusion.6), kind=kOutput, calls=%fused_computation.4.clone.1 | convolution fusion | flops 1296060416 | bytes 2141888 | tf_op jit(solution)/shard_map/while/body/eval_jaxpr/dot_general | solution.py:34
  30.9 4.2 %convolution_convert_fusion.4 = bf16[6400,16]{0,1:T(8,128)(2,1)S(1)} fusion(bf16[256,16]{0,1:T(8,128)(2,1)} %get-tuple-element.308, s32[6400]{0:T(1024)S(1)} %eq.56), kind=kOutput, calls=%fused_computation.5.clone.1 | convolution fusion | flops 54169600 | bytes 238592 | tf_op jit(solution)/shard_map/while/body/eval_jaxpr/dot_general | solution.py:23
  43.3 1.8 constant_dynamic-update-slice_fusion.33
  49.8 5.1 %select_reduce_fusion.2 = f32[128,896]{1,0:T(8,128)S(1)} fusion(pred[50,896]{1,0:T(8,128)(4,1)S(1)} %iota_compare_fusion.6, bf16[128,50,112]{0,2,1:T(8,128)(2,1)} %constant_dynamic-update-slice_fusion.36, bf16[112,896]{1,0:T(8,128)(2,1)} %get-tuple-element.309, s32[896]{0:T(1024)S(1)} %fusion.150, s32[112]{0:T(128)S(1)} %and_select_fusion.6), kind=kOutput, calls=%fused_computation.4.clone.1 | convolution fusion | flops 1296060416 | bytes 2141888 | tf_op jit(solution)/shard_map/while/body/eval_jaxpr/dot_general | solution.py:34
  59.1 4.2 %convolution_convert_fusion.4 = bf16[6400,16]{0,1:T(8,128)(2,1)S(1)} fusion(bf16[256,16]{0,1:T(8,128)(2,1)} %get-tuple-element.308, s32[6400]{0:T(1024)S(1)} %eq.56), kind=kOutput, calls=%fused_computation.5.clone.1 | convolution fusion | flops 54169600 | bytes 238592 | tf_op jit(solution)/shard_map/while/body/eval_jaxpr/dot_general | solution.py:23
  71.6 1.8 constant_dynamic-update-slice_fusion.33
  78.1 5.1 %select_reduce_fusion.2 = f32[128,896]{1,0:T(8,128)S(1)} fusion(pred[50,896]{1,0:T(8,128)(4,1)S(1)} %iota_compare_fusion.6, bf16[128,50,112]{0,2,1:T(8,128)(2,1)} %constant_dynamic-update-slice_fusion.36, bf16[112,896]{1,0:T(8,128)(2,1)} %get-tuple-element.309, s32[896]{0:T(1024)S(1)} %fusion.150, s32[112]{0:T(128)S(1)} %and_select_fusion.6), kind=kOutput, calls=%fused_computation.4.clone.1 | convolution fusion | flops 1296060416 | bytes 2141888 | tf_op jit(solution)/shard_map/while/body/eval_jaxpr/dot_general | solution.py:34
  87.4 4.2 %convolution_convert_fusion.4 = bf16[6400,16]{0,1:T(8,128)(2,1)S(1)} fusion(bf16[256,16]{0,1:T(8,128)(2,1)} %get-tuple-element.308, s32[6400]{0:T(1024)S(1)} %eq.56), kind=kOutput, calls=%fused_computation.5.clone.1 | convolution fusion | flops 54169600 | bytes 238592 | tf_op jit(solution)/shard_map/while/body/eval_jaxpr/dot_general | solution.py:23
  99.8 1.8 constant_dynamic-update-slice_fusion.33
  106.4 5.1 %select_reduce_fusion.2 = f32[128,896]{1,0:T(8,128)S(1)} fusion(pred[50,896]{1,0:T(8,128)(4,1)S(1)} %iota_compare_fusion.6, bf16[128,50,112]{0,2,1:T(8,128)(2,1)} %constant_dynamic-update-slice_fusion.36, bf16[112,896]{1,0:T(8,128)(2,1)} %get-tuple-element.309, s32[896]{0:T(1024)S(1)} %fusion.150, s32[112]{0:T(128)S(1)} %and_select_fusion.6), kind=kOutput, calls=%fused_computation.4.clone.1 | convolution fusion | flops 1296060416 | bytes 2141888 | tf_op jit(solution)/shard_map/while/body/eval_jaxpr/dot_general | solution.py:34
  115.3 15.6 %collective-permute-done = bf16[512,1024]{1,0:T(8,128)(2,1)S(1)} collective-permute-done((bf16[512,1024]{1,0:T(8,128)(2,1)}, bf16[512,1024]{1,0:T(8,128)(2,1)S(1)}, u32[]{:S(2)}, u32[]{:S(2)}) %collective-permute-start) | collective-permute-done | bytes 1048608 | tf_op jit(solution)/shard_map/ppermute | solution.py:134
  130.9 15.1 %collective-permute-done.1 = bf16[512,1024]{1,0:T(8,128)(2,1)S(1)} collective-permute-done((bf16[512,1024]{1,0:T(8,128)(2,1)S(1)}, bf16[512,1024]{1,0:T(8,128)(2,1)S(1)}, u32[]{:S(2)}, u32[]{:S(2)}) %collective-permute-start.1) | collective-permute-done | bytes 1048608 | tf_op jit(solution)/shard_map/ppermute | solution.py:134
  146.0 15.1 %collective-permute-done.2 = bf16[512,1024]{1,0:T(8,128)(2,1)S(1)} collective-permute-done((bf16[512,1024]{1,0:T(8,128)(2,1)S(1)}, bf16[512,1024]{1,0:T(8,128)(2,1)S(1)}, u32[]{:S(2)}, u32[]{:S(2)}) %collective-permute-start.2) | collective-permute-done | bytes 1048608 | tf_op jit(solution)/shard_map/ppermute | solution.py:134
  161.1 15.1 %collective-permute-done.3 = bf16[512,1024]{1,0:T(8,128)(2,1)S(1)} collective-permute-done((bf16[512,1024]{1,0:T(8,128)(2,1)S(1)}, bf16[512,1024]{1,0:T(8,128)(2,1)S(1)}, u32[]{:S(2)}, u32[]{:S(2)}) %collective-permute-start.3) | collective-permute-done | bytes 1048608 | tf_op jit(solution)/shard_map/ppermute | solution.py:134
  177.3 15.1 %collective-permute-done.4 = bf16[512,1024]{1,0:T(8,128)(2,1)S(1)} collective-permute-done((bf16[512,1024]{1,0:T(8,128)(2,1)S(1)}, bf16[512,1024]{1,0:T(8,128)(2,1)S(1)}, u32[]{:S(2)}, u32[]{:S(2)}) %collective-permute-start.4) | collective-permute-done | bytes 1048608 | tf_op jit(solution)/shard_map/ppermute | solution.py:134
  193.4 15.2 %collective-permute-done.5 = bf16[512,1024]{1,0:T(8,128)(2,1)} collective-permute-done((bf16[512,1024]{1,0:T(8,128)(2,1)S(1)}, bf16[512,1024]{1,0:T(8,128)(2,1)}, u32[]{:S(2)}, u32[]{:S(2)}) %collective-permute-start.5) | collective-permute-done | bytes 1048608 | tf_op jit(solution)/shard_map/ppermute | solution.py:134
  210.1 9.2 %all-reduce.1 = s32[256]{0:T(256)S(1)} all-reduce(s32[256]{0:T(256)S(1)} %dynamic-update-slice), channel_id=1, replica_groups=mesh['vocab'=8,'blk'=4] {'blk'}, use_global_device_ids=true, to_apply=%add.1 | all-reduce | flops 256 | bytes 2048
  220.1 15.8 %all_gather.6 = bf16[256,1024]{1,0:T(8,128)(2,1)S(1)} all-gather(bf16[64,1024]{1,0:T(8,128)(2,1)} %param.20), channel_id=1, replica_groups=mesh['vocab'=8,'blk'=4] {'blk'}, dimensions={0}, use_global_device_ids=true | all-gather | bytes 655360 | tf_op jit(solution)/shard_map/all_gather | solution.py:140
  235.9 2.3 constant_dynamic-update-slice_fusion.22
  238.2 2.3 constant_dynamic-update-slice_fusion.21
  240.4 2.4 constant_dynamic-update-slice_fusion.20
  242.8 2.3 constant_dynamic-update-slice_fusion.19
  249.5 2.4 constant_dynamic-update-slice_fusion.14
  251.8 2.3 constant_dynamic-update-slice_fusion.13
  260.5 7.6 %constant_dynamic-slice_fusion.1 = bf16[4096,1024]{1,0:T(8,128)(2,1)} fusion(bf16[8192,1024]{1,0:T(8,128)(2,1)} %constant_dynamic-update-slice_fusion.7, s32[]{:T(128)S(6)} %select_n.142), kind=kLoop, calls=%fused_computation.148 | loop fusion | bytes 16777220 | tf_op jit(solution)/shard_map/jit(_roll_dynamic)/dynamic_slice | solution.py:139
  268.2 7.3 %fusion.101 = (f32[64]{0:T(128)S(1)}, f32[64,4096]{1,0:T(8,128)}) fusion(bf16[4096,1024]{1,0:T(8,128)(2,1)} %constant_dynamic-slice_fusion.1, bf16[256,1024]{1,0:T(8,128)(2,1)S(1)} %all_gather.6, s32[]{:T(128)S(6)} %select_n.140), kind=kOutput, calls=%fused_computation.164 | convolution fusion | flops 537132992 | bytes 9568516 | tf_op jit(solution)/shard_map/dot_general | solution.py:91
  275.5 3.3 fusion.102
  278.8 3.3 fusion.103
  282.1 3.3 fusion.104
  285.4 5.3 %gather_fusion = bf16[64,1024]{1,0:T(8,128)(2,1)S(1)} fusion(bf16[4096,1024]{1,0:T(8,128)(2,1)} %constant_dynamic-slice_fusion.1, s32[1024]{0:T(1024)S(1)} %pad_clamp_fusion.3), kind=kCustom, calls=%fused_computation.clone | custom fusion | bytes 262400 | tf_op jit(solution)/shard_map/jit(_take)/gather | solution.py:83
  291.5 5.3 %gather_fusion.1 = bf16[64,1024]{1,0:T(8,128)(2,1)S(1)} fusion(bf16[4096,1024]{1,0:T(8,128)(2,1)} %constant_dynamic-slice_fusion.1, s32[1024]{0:T(1024)S(1)} %pad_clamp_fusion.2), kind=kCustom, calls=%fused_computation.1.clone | custom fusion | bytes 262400 | tf_op jit(solution)/shard_map/jit(_take)/gather | solution.py:83
  300.2 6.1 %convolution_add_fusion = f32[64,1024]{1,0:T(8,128)} fusion(bf16[4096,1024]{1,0:T(8,128)(2,1)} %constant_dynamic-slice_fusion.1, f32[64]{0:T(128)S(1)} %get-tuple-element.204, f32[64,4096]{1,0:T(8,128)} %get-tuple-element.207, f32[64]{0:T(128)S(1)} %get-tuple-element.206), kind=kOutput, calls=%fused_computation.76 | convolution fusion | flops 537460736 | bytes 9699840 | tf_op jit(solution)/shard_map/dot_general | solution.py:98
  306.3 5.3 %gather_fusion.2 = bf16[64,1024]{1,0:T(8,128)(2,1)S(1)} fusion(bf16[4096,1024]{1,0:T(8,128)(2,1)} %constant_dynamic-slice_fusion.1, s32[1024]{0:T(1024)S(1)} %pad_clamp_fusion.1), kind=kCustom, calls=%fused_computation.2.clone | custom fusion | bytes 262400 | tf_op jit(solution)/shard_map/jit(_take)/gather | solution.py:83
  311.5 5.3 %gather_fusion.3 = bf16[64,1024]{1,0:T(8,128)(2,1)S(1)} fusion(bf16[4096,1024]{1,0:T(8,128)(2,1)} %constant_dynamic-slice_fusion.1, s32[1024]{0:T(1024)S(1)} %pad_clamp_fusion), kind=kCustom, calls=%fused_computation.3.clone | custom fusion | bytes 262400 | tf_op jit(solution)/shard_map/jit(_take)/gather | solution.py:83
  318.4 2.1 collective-permute-start.11
  321.5 3.7 %collective-permute-done.11 = f32[64]{0:T(128)S(1)} collective-permute-done((f32[64]{0:T(128)}, f32[64]{0:T(128)S(1)}, u32[]{:S(2)}, u32[]{:S(2)}) %collective-permute-start.11) | collective-permute-done | bytes 288 | tf_op jit(solution)/shard_map/ppermute | solution.py:10
  329.1 2.1 collective-permute-done.12
  334.3 5.2 %multiply_add_fusion.2 = f32[64,1024]{1,0:T(8,128)S(1)} fusion(f32[64,1024]{1,0:T(8,128)S(1)} %collective-permute-done.19, f32[64]{0:T(128)S(1)} %get-tuple-element.173, bf16[4096,1024]{1,0:T(8,128)(2,1)} %constant_dynamic-slice_fusion.1, f32[64,4096]{1,0:T(8,128)S(1)} %get-tuple-element.209, f32[64]{0:T(128)S(1)} %max.43), kind=kOutput, calls=%fused_computation.88 | convolution fusion | flops 537526272 | bytes 9961984 | tf_op jit(solution)/shard_map/dot_general | solution.py:98
  340.1 3.5 collective-permute-done.16
  343.8 6.8 %collective-permute-done.20 = f32[64,1024]{1,0:T(8,128)S(1)} collective-permute-done((f32[64,1024]{1,0:T(8,128)S(1)}, f32[64,1024]{1,0:T(8,128)S(1)}, u32[]{:S(2)}, u32[]{:S(2)}) %collective-permute-start.20) | collective-permute-done | bytes 262176 | tf_op jit(solution)/shard_map/ppermute | solution.py:10
  350.6 1.7 multiply_add_fusion.1
  352.4 3.1 collective-permute-done.17
  355.7 4.8 %collective-permute-done.21 = f32[64,1024]{1,0:T(8,128)S(1)} collective-permute-done((f32[64,1024]{1,0:T(8,128)S(1)}, f32[64,1024]{1,0:T(8,128)S(1)}, u32[]{:S(2)}, u32[]{:S(2)}) %collective-permute-start.21) | collective-permute-done | bytes 262176 | tf_op jit(solution)/shard_map/ppermute | solution.py:10
  360.6 1.7 multiply_add_fusion
  363.6 6.9 %collective-permute-done.14 = f32[64]{0:T(128)S(1)} collective-permute-done((f32[64]{0:T(128)S(1)}, f32[64]{0:T(128)S(1)}, u32[]{:S(2)}, u32[]{:S(2)}) %collective-permute-start.14) | collective-permute-done | bytes 288 | tf_op jit(solution)/shard_map/ppermute | solution.py:10
  (255 shorter events, 101.5 us)
Async XLA Ops:
  1.7 206.9 %copy-start.17 = (u32[32]{0:T(128)S(1)}, u32[32]{0:T(128)}, u32[]{:S(2)}) copy-start(u32[32]{0:T(128)} %constant.248) | copy-start | bytes 388
  1.7 208.2 %copy-start.16 = (s32[64]{0:T(128)S(1)}, s32[64]{0:T(128)}, u32[]{:S(2)}) copy-start(s32[64]{0:T(128)} %param.21) | copy-start | bytes 772
  15.0 11.7 %copy-start.1 = (bf16[896,1024]{1,0:T(8,128)(2,1)S(1)}, bf16[896,1024]{1,0:T(8,128)(2,1)}, u32[]{:S(2)}) copy-start(bf16[896,1024]{1,0:T(8,128)(2,1)} %get-tuple-element.310) | copy-start | bytes 5505028 | tf_op jit(solution)/shard_map/while
  19.5 7.7 %copy-start.10 = (f32[2,1024]{1,0:T(2,128)S(1)}, f32[2,1024]{1,0:T(2,128)}, u32[]{:S(2)}) copy-start(f32[2,1024]{1,0:T(2,128)} %get-tuple-element.312) | copy-start | bytes 24580 | tf_op jit(solution)/shard_map/while
  20.8 6.4 %copy-start.14 = (bf16[2,1024,1024]{2,1,0:T(8,128)(2,1)S(1)}, bf16[2,1024,1024]{2,1,0:T(8,128)(2,1)}, u32[]{:S(2)}) copy-start(bf16[2,1024,1024]{2,1,0:T(8,128)(2,1)} %get-tuple-element.311) | copy-start | bytes 12582916 | tf_op jit(solution)/shard_map/while
  21.5 6.2 %copy-start.15 = (bf16[2,1024,1024]{2,1,0:T(8,128)(2,1)S(1)}, bf16[2,1024,1024]{2,1,0:T(8,128)(2,1)}, u32[]{:S(2)}) copy-start(bf16[2,1024,1024]{2,1,0:T(8,128)(2,1)} %get-tuple-element.313) | copy-start | bytes 12582916 | tf_op jit(solution)/shard_map/while
  43.3 11.7 %copy-start.1 = (bf16[896,1024]{1,0:T(8,128)(2,1)S(1)}, bf16[896,1024]{1,0:T(8,128)(2,1)}, u32[]{:S(2)}) copy-start(bf16[896,1024]{1,0:T(8,128)(2,1)} %get-tuple-element.310) | copy-start | bytes 5505028 | tf_op jit(solution)/shard_map/while
  47.8 7.7 %copy-start.10 = (f32[2,1024]{1,0:T(2,128)S(1)}, f32[2,1024]{1,0:T(2,128)}, u32[]{:S(2)}) copy-start(f32[2,1024]{1,0:T(2,128)} %get-tuple-element.312) | copy-start | bytes 24580 | tf_op jit(solution)/shard_map/while
  49.1 6.4 %copy-start.14 = (bf16[2,1024,1024]{2,1,0:T(8,128)(2,1)S(1)}, bf16[2,1024,1024]{2,1,0:T(8,128)(2,1)}, u32[]{:S(2)}) copy-start(bf16[2,1024,1024]{2,1,0:T(8,128)(2,1)} %get-tuple-element.311) | copy-start | bytes 12582916 | tf_op jit(solution)/shard_map/while
  71.6 11.7 %copy-start.1 = (bf16[896,1024]{1,0:T(8,128)(2,1)S(1)}, bf16[896,1024]{1,0:T(8,128)(2,1)}, u32[]{:S(2)}) copy-start(bf16[896,1024]{1,0:T(8,128)(2,1)} %get-tuple-element.310) | copy-start | bytes 5505028 | tf_op jit(solution)/shard_map/while
  76.0 7.7 %copy-start.10 = (f32[2,1024]{1,0:T(2,128)S(1)}, f32[2,1024]{1,0:T(2,128)}, u32[]{:S(2)}) copy-start(f32[2,1024]{1,0:T(2,128)} %get-tuple-element.312) | copy-start | bytes 24580 | tf_op jit(solution)/shard_map/while
  77.4 6.4 %copy-start.14 = (bf16[2,1024,1024]{2,1,0:T(8,128)(2,1)S(1)}, bf16[2,1024,1024]{2,1,0:T(8,128)(2,1)}, u32[]{:S(2)}) copy-start(bf16[2,1024,1024]{2,1,0:T(8,128)(2,1)} %get-tuple-element.311) | copy-start | bytes 12582916 | tf_op jit(solution)/shard_map/while
  78.1 6.2 %copy-start.15 = (bf16[2,1024,1024]{2,1,0:T(8,128)(2,1)S(1)}, bf16[2,1024,1024]{2,1,0:T(8,128)(2,1)}, u32[]{:S(2)}) copy-start(bf16[2,1024,1024]{2,1,0:T(8,128)(2,1)} %get-tuple-element.313) | copy-start | bytes 12582916 | tf_op jit(solution)/shard_map/while
  99.8 11.7 %copy-start.1 = (bf16[896,1024]{1,0:T(8,128)(2,1)S(1)}, bf16[896,1024]{1,0:T(8,128)(2,1)}, u32[]{:S(2)}) copy-start(bf16[896,1024]{1,0:T(8,128)(2,1)} %get-tuple-element.310) | copy-start | bytes 5505028 | tf_op jit(solution)/shard_map/while
  104.3 7.7 %copy-start.10 = (f32[2,1024]{1,0:T(2,128)S(1)}, f32[2,1024]{1,0:T(2,128)}, u32[]{:S(2)}) copy-start(f32[2,1024]{1,0:T(2,128)} %get-tuple-element.312) | copy-start | bytes 24580 | tf_op jit(solution)/shard_map/while
  105.6 6.4 %copy-start.14 = (bf16[2,1024,1024]{2,1,0:T(8,128)(2,1)S(1)}, bf16[2,1024,1024]{2,1,0:T(8,128)(2,1)}, u32[]{:S(2)}) copy-start(bf16[2,1024,1024]{2,1,0:T(8,128)(2,1)} %get-tuple-element.311) | copy-start | bytes 12582916 | tf_op jit(solution)/shard_map/while
  114.9 16.0 %collective-permute-start = (bf16[512,1024]{1,0:T(8,128)(2,1)}, bf16[512,1024]{1,0:T(8,128)(2,1)S(1)}, u32[]{:S(2)}, u32[]{:S(2)}) collective-permute-start(bf16[512,1024]{1,0:T(8,128)(2,1)} %bitcast.113), channel_id=1, source_target_pairs={{0,4},{4,8},{8,12},{12,16},{16,20},{20,24},{24,28},{28,0},{1,5},{5... | collective-permute-start | bytes 3145736 | tf_op jit(solution)/shard_map/ppermute | solution.py:134
  130.9 15.1 %collective-permute-start.1 = (bf16[512,1024]{1,0:T(8,128)(2,1)S(1)}, bf16[512,1024]{1,0:T(8,128)(2,1)S(1)}, u32[]{:S(2)}, u32[]{:S(2)}) collective-permute-start(bf16[512,1024]{1,0:T(8,128)(2,1)S(1)} %collective-permute-done), channel_id=1, source_target_pairs={{0,4},{4,8},{8,12},{12,16},{16,20},{20,24},{24,28},{28,0},{1,5},{5... | collective-permute-start | bytes 3145736 | tf_op jit(solution)/shard_map/ppermute | solution.py:134
  146.0 15.1 %collective-permute-start.2 = (bf16[512,1024]{1,0:T(8,128)(2,1)S(1)}, bf16[512,1024]{1,0:T(8,128)(2,1)S(1)}, u32[]{:S(2)}, u32[]{:S(2)}) collective-permute-start(bf16[512,1024]{1,0:T(8,128)(2,1)S(1)} %collective-permute-done.1), channel_id=1, source_target_pairs={{0,4},{4,8},{8,12},{12,16},{16,20},{20,24},{24,28},{28,0},{1,5},{5... | collective-permute-start | bytes 3145736 | tf_op jit(solution)/shard_map/ppermute | solution.py:134
  161.1 15.1 %collective-permute-start.3 = (bf16[512,1024]{1,0:T(8,128)(2,1)S(1)}, bf16[512,1024]{1,0:T(8,128)(2,1)S(1)}, u32[]{:S(2)}, u32[]{:S(2)}) collective-permute-start(bf16[512,1024]{1,0:T(8,128)(2,1)S(1)} %collective-permute-done.2), channel_id=1, source_target_pairs={{0,4},{4,8},{8,12},{12,16},{16,20},{20,24},{24,28},{28,0},{1,5},{5... | collective-permute-start | bytes 3145736 | tf_op jit(solution)/shard_map/ppermute | solution.py:134
  177.3 15.1 %collective-permute-start.4 = (bf16[512,1024]{1,0:T(8,128)(2,1)S(1)}, bf16[512,1024]{1,0:T(8,128)(2,1)S(1)}, u32[]{:S(2)}, u32[]{:S(2)}) collective-permute-start(bf16[512,1024]{1,0:T(8,128)(2,1)S(1)} %collective-permute-done.3), channel_id=1, source_target_pairs={{0,4},{4,8},{8,12},{12,16},{16,20},{20,24},{24,28},{28,0},{1,5},{5... | collective-permute-start | bytes 3145736 | tf_op jit(solution)/shard_map/ppermute | solution.py:134
  193.4 15.2 %collective-permute-start.5 = (bf16[512,1024]{1,0:T(8,128)(2,1)S(1)}, bf16[512,1024]{1,0:T(8,128)(2,1)}, u32[]{:S(2)}, u32[]{:S(2)}) collective-permute-start(bf16[512,1024]{1,0:T(8,128)(2,1)S(1)} %collective-permute-done.4), channel_id=1, source_target_pairs={{0,4},{4,8},{8,12},{12,16},{16,20},{20,24},{24,28},{28,0},{1,5},{5... | collective-permute-start | bytes 3145736 | tf_op jit(solution)/shard_map/ppermute | solution.py:134
  208.6 27.3 %collective-permute-start.6 = (bf16[512,1024]{1,0:T(8,128)(2,1)}, bf16[512,1024]{1,0:T(8,128)(2,1)}, u32[]{:S(2)}, u32[]{:S(2)}) collective-permute-start(bf16[512,1024]{1,0:T(8,128)(2,1)} %collective-permute-done.5), channel_id=1, source_target_pairs={{0,4},{4,8},{8,12},{12,16},{16,20},{20,24},{24,28},{28,0},{1,5},{5... | collective-permute-start | bytes 3145736 | tf_op jit(solution)/shard_map/ppermute | solution.py:134
  219.3 29.0 %copy-start.6 = (bf16[4,128,1024]{2,1,0:T(8,128)(2,1)S(1)}, bf16[4,128,1024]{2,1,0:T(8,128)(2,1)}, u32[]{:S(2)}) copy-start(bf16[4,128,1024]{2,1,0:T(8,128)(2,1)} %get-tuple-element.149) | copy-start | bytes 3145732
  240.4 13.7 %copy-start.5 = (bf16[512,1024]{1,0:T(8,128)(2,1)S(1)}, bf16[512,1024]{1,0:T(8,128)(2,1)}, u32[]{:S(2)}) copy-start(bf16[512,1024]{1,0:T(8,128)(2,1)} %copy-done.4) | copy-start | bytes 3145732
  242.8 12.4 %copy-start.3 = (bf16[512,1024]{1,0:T(8,128)(2,1)S(1)}, bf16[512,1024]{1,0:T(8,128)(2,1)}, u32[]{:S(2)}) copy-start(bf16[512,1024]{1,0:T(8,128)(2,1)} %copy-done.2) | copy-start | bytes 3145732
  268.2 7.3 %copy-start = (bf16[4096,1024]{1,0:T(8,128)(2,1)S(1)}, bf16[4096,1024]{1,0:T(8,128)(2,1)}, u32[]{:S(2)}) copy-start(bf16[4096,1024]{1,0:T(8,128)(2,1)} %constant_dynamic-slice_fusion.1) | copy-start | bytes 25165828
  291.5 41.7 %collective-permute-start.15 = (f32[64,1024]{1,0:T(8,128)}, f32[64,1024]{1,0:T(8,128)}, u32[]{:S(2)}, u32[]{:S(2)}) collective-permute-start(f32[64,1024]{1,0:T(8,128)} %convert_select_fusion), channel_id=1, source_target_pairs={{0,1},{1,2},{2,3},{3,0},{4,5},{5,6},{6,7},{7,4},{8,9},{9,10},{10,1... | collective-permute-start | bytes 786440 | tf_op jit(solution)/shard_map/ppermute | solution.py:10
  296.8 23.7 %collective-permute-start.7 = (f32[64]{0:T(128)S(1)}, f32[64]{0:T(128)}, u32[]{:S(2)}, u32[]{:S(2)}) collective-permute-start(f32[64]{0:T(128)S(1)} %get-tuple-element.206), channel_id=1, source_target_pairs={{0,1},{1,2},{2,3},{3,0},{4,5},{5,6},{6,7},{7,4},{8,9},{9,10},{10,1... | collective-permute-start | bytes 776 | tf_op jit(solution)/shard_map/ppermute | solution.py:10
  316.8 17.5 %collective-permute-start.19 = (f32[64,1024]{1,0:T(8,128)}, f32[64,1024]{1,0:T(8,128)S(1)}, u32[]{:S(2)}, u32[]{:S(2)}) collective-permute-start(f32[64,1024]{1,0:T(8,128)} %convolution_add_fusion), channel_id=1, source_target_pairs={{0,1},{1,2},{2,3},{3,0},{4,5},{5,6},{6,7},{7,4},{8,9},{9,10},{10,1... | collective-permute-start | bytes 786440 | tf_op jit(solution)/shard_map/ppermute | solution.py:10
  318.4 6.9 %collective-permute-start.11 = (f32[64]{0:T(128)}, f32[64]{0:T(128)S(1)}, u32[]{:S(2)}, u32[]{:S(2)}) collective-permute-start(f32[64]{0:T(128)} %get-tuple-element.205), channel_id=1, source_target_pairs={{0,1},{1,2},{2,3},{3,0},{4,5},{5,6},{6,7},{7,4},{8,9},{9,10},{10,1... | collective-permute-start | bytes 776 | tf_op jit(solution)/shard_map/ppermute | solution.py:10
  321.2 5.3 %collective-permute-start.8 = (f32[64]{0:T(128)S(1)}, f32[64]{0:T(128)S(1)}, u32[]{:S(2)}, u32[]{:S(2)}) collective-permute-start(f32[64]{0:T(128)S(1)} %max.43), channel_id=1, source_target_pairs={{0,1},{1,2},{2,3},{3,0},{4,5},{5,6},{6,7},{7,4},{8,9},{9,10},{10,1... | collective-permute-start | bytes 776 | tf_op jit(solution)/shard_map/ppermute | solution.py:10
  325.9 5.3 %collective-permute-start.12 = (f32[64]{0:T(128)S(1)}, f32[64]{0:T(128)S(1)}, u32[]{:S(2)}, u32[]{:S(2)}) collective-permute-start(f32[64]{0:T(128)S(1)} %get-tuple-element.172), channel_id=1, source_target_pairs={{0,1},{1,2},{2,3},{3,0},{4,5},{5,6},{6,7},{7,4},{8,9},{9,10},{10,1... | collective-permute-start | bytes 776 | tf_op jit(solution)/shard_map/ppermute | solution.py:10
  327.2 5.3 %collective-permute-start.9 = (f32[64]{0:T(128)S(1)}, f32[64]{0:T(128)S(1)}, u32[]{:S(2)}, u32[]{:S(2)}) collective-permute-start(f32[64]{0:T(128)S(1)} %max.44), channel_id=1, source_target_pairs={{0,1},{1,2},{2,3},{3,0},{4,5},{5,6},{6,7},{7,4},{8,9},{9,10},{10,1... | collective-permute-start | bytes 776 | tf_op jit(solution)/shard_map/ppermute | solution.py:10
  328.8 21.8 %slice-start = ((s8[8388608]{0:T(1024)(128)(4,1)}), s8[4194304]{0:T(1024)(128)(4,1)S(1)}, s32[]{:S(2)}) async-start(s8[8388608]{0:T(1024)(128)(4,1)} %bitcast.111), calls=%async_computation | async-start | bytes 8388608
  331.2 21.2 %collective-permute-start.13 = (f32[64]{0:T(128)S(1)}, f32[64]{0:T(128)S(1)}, u32[]{:S(2)}, u32[]{:S(2)}) collective-permute-start(f32[64]{0:T(128)S(1)} %get-tuple-element.170), channel_id=1, source_target_pairs={{0,1},{1,2},{2,3},{3,0},{4,5},{5,6},{6,7},{7,4},{8,9},{9,10},{10,1... | collective-permute-start | bytes 776 | tf_op jit(solution)/shard_map/ppermute | solution.py:10
  334.2 9.4 %collective-permute-start.16 = (f32[64,1024]{1,0:T(8,128)S(1)}, f32[64,1024]{1,0:T(8,128)S(1)}, u32[]{:S(2)}, u32[]{:S(2)}) collective-permute-start(f32[64,1024]{1,0:T(8,128)S(1)} %select_add_fusion.2), channel_id=1, source_target_pairs={{0,1},{1,2},{2,3},{3,0},{4,5},{5,6},{6,7},{7,4},{8,9},{9,10},{10,1... | collective-permute-start | bytes 786440 | tf_op jit(solution)/shard_map/ppermute | solution.py:10
  334.3 9.3 %copy-start.12 = (pred[64]{0:T(512)(128)(4,1)S(1)}, pred[64]{0:T(512)(128)(4,1)}, u32[]{:S(2)}) copy-start(pred[64]{0:T(512)(128)(4,1)} %get-tuple-element.195) | copy-start | bytes 196
  334.3 9.3 %copy-start.13 = (pred[64]{0:T(512)(128)(4,1)S(1)}, pred[64]{0:T(512)(128)(4,1)}, u32[]{:S(2)}) copy-start(pred[64]{0:T(512)(128)(4,1)} %get-tuple-element.198) | copy-start | bytes 196
  334.3 16.3 %slice-start.1 = ((s8[8388608]{0:T(1024)(128)(4,1)}), s8[4194304]{0:T(1024)(128)(4,1)S(1)}, s32[]{:S(2)}) async-start(s8[8388608]{0:T(1024)(128)(4,1)} %bitcast.111), calls=%async_computation.1 | async-start | bytes 8388608
  339.5 11.1 %collective-permute-start.20 = (f32[64,1024]{1,0:T(8,128)S(1)}, f32[64,1024]{1,0:T(8,128)S(1)}, u32[]{:S(2)}, u32[]{:S(2)}) collective-permute-start(f32[64,1024]{1,0:T(8,128)S(1)} %multiply_add_fusion.2), channel_id=1, source_target_pairs={{0,1},{1,2},{2,3},{3,0},{4,5},{5,6},{6,7},{7,4},{8,9},{9,10},{10,1... | collective-permute-start | bytes 786440 | tf_op jit(solution)/shard_map/ppermute | solution.py:10
  343.8 11.8 %collective-permute-start.17 = (f32[64,1024]{1,0:T(8,128)S(1)}, f32[64,1024]{1,0:T(8,128)S(1)}, u32[]{:S(2)}, u32[]{:S(2)}) collective-permute-start(f32[64,1024]{1,0:T(8,128)S(1)} %select_add_fusion.1), channel_id=1, source_target_pairs={{0,1},{1,2},{2,3},{3,0},{4,5},{5,6},{6,7},{7,4},{8,9},{9,10},{10,1... | collective-permute-start | bytes 786440 | tf_op jit(solution)/shard_map/ppermute | solution.py:10
  352.3 8.2 %collective-permute-start.21 = (f32[64,1024]{1,0:T(8,128)S(1)}, f32[64,1024]{1,0:T(8,128)S(1)}, u32[]{:S(2)}, u32[]{:S(2)}) collective-permute-start(f32[64,1024]{1,0:T(8,128)S(1)} %multiply_add_fusion.1), channel_id=1, source_target_pairs={{0,1},{1,2},{2,3},{3,0},{4,5},{5,6},{6,7},{7,4},{8,9},{9,10},{10,1... | collective-permute-start | bytes 786440 | tf_op jit(solution)/shard_map/ppermute | solution.py:10
  355.6 14.9 %collective-permute-start.18 = (f32[64,1024]{1,0:T(8,128)S(1)}, f32[64,1024]{1,0:T(8,128)S(1)}, u32[]{:S(2)}, u32[]{:S(2)}) collective-permute-start(f32[64,1024]{1,0:T(8,128)S(1)} %select_add_fusion), channel_id=1, source_target_pairs={{0,1},{1,2},{2,3},{3,0},{4,5},{5,6},{6,7},{7,4},{8,9},{9,10},{10,1... | collective-permute-start | bytes 786440 | tf_op jit(solution)/shard_map/ppermute | solution.py:10
  360.6 10.0 %copy-start.9 = (bf16[64,1024]{1,0:T(8,128)(2,1)S(1)}, bf16[64,1024]{1,0:T(8,128)(2,1)}, u32[]{:S(2)}) copy-start(bf16[64,1024]{1,0:T(8,128)(2,1)} %param.20) | copy-start | bytes 393220
  362.3 8.3 %collective-permute-start.22 = (f32[64,1024]{1,0:T(8,128)S(1)}, f32[64,1024]{1,0:T(8,128)S(1)}, u32[]{:S(2)}, u32[]{:S(2)}) collective-permute-start(f32[64,1024]{1,0:T(8,128)S(1)} %multiply_add_fusion), channel_id=1, source_target_pairs={{0,1},{1,2},{2,3},{3,0},{4,5},{5,6},{6,7},{7,4},{8,9},{9,10},{10,1... | collective-permute-start | bytes 786440 | tf_op jit(solution)/shard_map/ppermute | solution.py:10
  362.3 8.2 %collective-permute-start.14 = (f32[64]{0:T(128)S(1)}, f32[64]{0:T(128)S(1)}, u32[]{:S(2)}, u32[]{:S(2)}) collective-permute-start(f32[64]{0:T(128)S(1)} %get-tuple-element.168), channel_id=1, source_target_pairs={{0,1},{1,2},{2,3},{3,0},{4,5},{5,6},{6,7},{7,4},{8,9},{9,10},{10,1... | collective-permute-start | bytes 776 | tf_op jit(solution)/shard_map/ppermute | solution.py:10
  362.4 9.0 %collective-permute-start.10 = (f32[64]{0:T(128)S(1)}, f32[64]{0:T(128)S(1)}, u32[]{:S(2)}, u32[]{:S(2)}) collective-permute-start(f32[64]{0:T(128)S(1)} %max.45), channel_id=1, source_target_pairs={{0,1},{1,2},{2,3},{3,0},{4,5},{5,6},{6,7},{7,4},{8,9},{9,10},{10,1... | collective-permute-start | bytes 776 | tf_op jit(solution)/shard_map/ppermute | solution.py:10
  (13 other events, 33.4 us)
